TPU v7x, 32 devices: a whole 2x2x4 slice. The times are simulated.
32 devices in a mesh: row: 16 (over z, y, core), col: 2 (over x).
Axes of the slice: x: 2, y: 2, z: 4, core: 2. Of those that a mesh axis runs over, the one named last changes fastest.
Arguments:
- layer_input: bfloat16 [16384, 1152], P(('row', 'col')), may hold values from -6 to 6
- attn_gain: bfloat16 [1152], replicated, may hold values from 0.099609375 to 1.8984375
- mlp_gain: bfloat16 [1152], replicated, may hold values from 0.099609375 to 1.8984375
- query_weight: bfloat16 [1152, 1152], P('row', 'col'), may hold values from -0.1875 to 0.1875
- key_weight: bfloat16 [1152, 384], P('row', 'col'), may hold values from -0.1875 to 0.1875
- value_weight: bfloat16 [1152, 384], P('row', 'col'), may hold values from -0.1875 to 0.1875
- out_weight: bfloat16 [1152, 1152], P('col', 'row'), may hold values from -4 to 4
- gate_weight: bfloat16 [1152, 3072], P('row', 'col'), may hold values from -0.1875 to 0.1875
- up_weight: bfloat16 [1152, 3072], P('row', 'col'), may hold values from -0.1875 to 0.1875
- down_weight: bfloat16 [3072, 1152], P('col', 'row'), may hold values from -0.109375 to 0.109375
- seq_ids: int32 [16384], P('row'), may hold values from 0 to 31, as said below
- block_ends: int32 [16384], P('row'), may hold values from 255 to 16383, as said below
- grad_output: bfloat16 [16384, 1152], P(('row', 'col')), may hold values from -6 to 6
Outputs:
- layer_output: bfloat16 [16384, 1152], P(('row', 'col'))
- grad_input: bfloat16 [16384, 1152], P(('row', 'col'))
- grad_attn_gain: float32 [1152], replicated
- grad_mlp_gain: float32 [1152], replicated
- grad_query: float32 [1152, 1152], P('row', 'col')
- grad_key: float32 [1152, 384], P('row', 'col')
- grad_value: float32 [1152, 384], P('row', 'col')
- grad_out_weight: float32 [1152, 1152], P('col', 'row')
- grad_gate: float32 [1152, 3072], P('row', 'col')
- grad_up: float32 [1152, 3072], P('row', 'col')
- grad_down: float32 [3072, 1152], P('col', 'row')
Inputs may be any that keep to these rules, and one draw needn't show every extreme that they name: `seq_ids`: ids never fall; span number s of the aligned spans of 1024 tokens holds exactly two sequences, with ids 2 * s and 2 * s + 1, each of 256 tokens or more. `block_ends`: values never fall; an attention block is a run of 1 to 256 tokens inside one sequence, and the first block of every sequence has exactly 256 tokens.
All inputs are finite; a program needn't handle non-finite values.
Results may differ from a plain program's by a relative error of at most 0.014.
The roundings to bfloat16 on the way count: a program that leaves them out, or rounds other values in their place, can miss the bound.
Values may be sent and summed in bfloat16 or wider, within the bound.
A program may use at most 192 MiB of HBM per device.

v0:
```python
import math
import jax
import jax.numpy as jnp
from jax import lax
from jax.sharding import PartitionSpec as P

QUERY_HEADS = 18
KEY_VALUE_HEADS = 6
HEAD_SIZE_DIM = 64
eps = 1e-05
rope_base = 10000.0
neg_fill = -1e30


def rotate_half(values, head_size):
    lane_index = jnp.arange(values.shape[-1], dtype=jnp.int32) % head_size
    forward_roll = jnp.roll(values, -(head_size // 2), axis=-1)
    backward_roll = jnp.roll(values, head_size // 2, axis=-1)
    return jnp.where(lane_index < head_size // 2, -forward_roll, backward_roll)


def rope_tables(position, table_width, head_size):
    lane_index = (jnp.arange(table_width, dtype=jnp.int32) % (head_size // 2)).astype(jnp.float32)
    frequency = jnp.exp(lane_index * (-2.0 * math.log(rope_base) / head_size))
    angles = position[:, None] * frequency[None, :]
    return (jnp.cos(angles), jnp.sin(angles))


def rotary(values, cosine, sine_part, head_size):
    return values * cosine + rotate_half(values, head_size) * sine_part


def rotary_back(upstream, cosine, sine_part, head_size):
    return upstream * cosine - rotate_half(upstream * sine_part, head_size)


def positions(seq_ids):
    token_index = jnp.arange(seq_ids.shape[0], dtype=jnp.int32)
    earlier = jnp.concatenate([seq_ids[:1] - 1, seq_ids[:-1]])
    seq_start = lax.cummax(jnp.where(seq_ids != earlier, token_index, 0), axis=0)
    return (token_index - seq_start).astype(jnp.float32)


def visible(query_seq, query_end, seq_ids, block_ends):
    return (query_seq[:, None] == seq_ids[None, :]) & (block_ends[None, :] <= query_end[:, None])


def to_rows(values):
    return lax.all_to_all(values, "col", split_axis=0, concat_axis=1, tiled=True)


def to_tokens(values):
    return lax.all_to_all(values, "col", split_axis=1, concat_axis=0, tiled=True)


def col_sums(values):
    return lax.psum_scatter(values, "col", scatter_dimension=0, tiled=True)


def widen(values):
    return lax.all_gather(values, "col", axis=0, tiled=True)


def shards(
    layer_input,
    attn_gain,
    mlp_gain,
    query_weight,
    key_weight,
    value_weight,
    out_weight,
    gate_weight,
    up_weight,
    down_weight,
    seq_ids,
    block_ends,
    grad_output,
):
    col_index = lax.axis_index("col")
    query_rows = layer_input.shape[0]
    block_rows = min(512, query_rows)
    block_count = query_rows // block_rows
    heads_per_group = QUERY_HEADS // KEY_VALUE_HEADS
    group_head_width = heads_per_group * HEAD_SIZE_DIM
    query_width = QUERY_HEADS * HEAD_SIZE_DIM
    score_scale = HEAD_SIZE_DIM ** (-0.5)
    attn_gain_float = attn_gain.astype(jnp.float32)
    mlp_gain_float = mlp_gain.astype(jnp.float32)
    full_input = lax.all_gather(layer_input, "col", axis=0, tiled=True)
    token_rows = full_input.shape[0]
    query_cols, key_cols, value_cols, out_rows, gate_cols, up_cols, down_rows = (
        lax.all_gather(query_weight, "row", axis=0, tiled=True),
        lax.all_gather(key_weight, "row", axis=0, tiled=True),
        lax.all_gather(value_weight, "row", axis=0, tiled=True),
        lax.all_gather(out_weight, "row", axis=1, tiled=True),
        lax.all_gather(gate_weight, "row", axis=0, tiled=True),
        lax.all_gather(up_weight, "row", axis=0, tiled=True),
        lax.all_gather(down_weight, "row", axis=1, tiled=True),
    )
    input_float = full_input.astype(jnp.float32)
    inv_all = lax.rsqrt(jnp.mean(input_float * input_float, axis=1, keepdims=True) + eps)
    attn_in = (input_float * inv_all * attn_gain_float).astype(jnp.bfloat16)
    query_unrotated = jnp.dot(attn_in, query_cols, preferred_element_type=jnp.float32).astype(
        jnp.bfloat16
    )
    key_raw = jnp.dot(attn_in, key_cols, preferred_element_type=jnp.float32).astype(jnp.bfloat16)
    value_projected = jnp.dot(attn_in, value_cols, preferred_element_type=jnp.float32).astype(
        jnp.bfloat16
    )
    query_all = to_rows(query_unrotated)
    key_all, value_all = (
        lax.all_gather(key_raw, "col", axis=1, tiled=True),
        lax.all_gather(value_projected, "col", axis=1, tiled=True),
    )
    position = positions(seq_ids)
    row_start = col_index * query_rows
    query_pos = lax.dynamic_slice_in_dim(position, row_start, query_rows)
    query_seq = lax.dynamic_slice_in_dim(seq_ids, row_start, query_rows)
    query_end = lax.dynamic_slice_in_dim(block_ends, row_start, query_rows)
    query_cos, query_sin = rope_tables(query_pos, query_width, HEAD_SIZE_DIM)
    key_cos, key_sin = rope_tables(position, key_all.shape[1], HEAD_SIZE_DIM)
    query_rotated = (
        rotary(query_all.astype(jnp.float32), query_cos, query_sin, HEAD_SIZE_DIM) * score_scale
    ).astype(jnp.bfloat16)
    key_rotated = rotary(key_all.astype(jnp.float32), key_cos, key_sin, HEAD_SIZE_DIM).astype(
        jnp.bfloat16
    )

    def block_inputs(block_index):
        first_row = block_index * block_rows
        allowed = visible(query_seq, query_end, seq_ids, block_ends)
        return (first_row, allowed)

    def group_scores(query_block, group_index, allowed):
        query_head_rows = lax.dynamic_slice_in_dim(
            query_block, group_index * group_head_width, group_head_width, 1
        ).reshape(block_rows, heads_per_group, HEAD_SIZE_DIM)
        key_group = lax.dynamic_slice_in_dim(
            key_rotated, group_index * HEAD_SIZE_DIM, HEAD_SIZE_DIM, 1
        )
        value_group = lax.dynamic_slice_in_dim(
            value_all, group_index * HEAD_SIZE_DIM, HEAD_SIZE_DIM, 1
        )
        scores = jnp.einsum(
            "qhd,kd->hqk", query_head_rows, key_group, preferred_element_type=jnp.float32
        )
        return (query_head_rows, key_group, value_group, jnp.where(allowed[None], scores, neg_fill))

    def attend_block(block_index):
        first_row, allowed = block_inputs(block_index)

        def attend_head_group(group_index):
            query_head_rows, key_group, value_group, scores = group_scores(
                query_rotated, group_index, allowed
            )
            row_top = jnp.max(scores, axis=2, keepdims=True)
            powers = jnp.exp(scores - row_top)
            exp_total = jnp.sum(powers, axis=2, keepdims=True)
            attn_probs = (powers / exp_total).astype(jnp.bfloat16)
            weighted_values = jnp.einsum(
                "hqk,kd->qhd", attn_probs, value_group, preferred_element_type=jnp.float32
            )
            return (
                weighted_values.reshape(block_rows, group_head_width),
                (row_top + jnp.log(exp_total))[:, :, 0],
            )

        weighted_value_rows, logsumexp_rows = lax.map(
            attend_head_group, jnp.arange(KEY_VALUE_HEADS, dtype=jnp.int32)
        )
        return (
            jnp.transpose(weighted_value_rows, (1, 0, 2)).reshape(block_rows, query_width),
            logsumexp_rows,
        )

    mixed_blocks, log_blocks = lax.map(attend_block, jnp.arange(block_count, dtype=jnp.int32))
    attn_rows = mixed_blocks.reshape(query_rows, query_width).astype(jnp.bfloat16)
    attn_tokens = to_tokens(attn_rows)
    attn_share = col_sums(jnp.dot(attn_tokens, out_rows, preferred_element_type=jnp.float32))
    residual = layer_input.astype(jnp.float32) + attn_share
    inv_two = lax.rsqrt(jnp.mean(residual * residual, axis=1, keepdims=True) + eps)
    normed_two = residual * inv_two
    mlp_in = widen((normed_two * mlp_gain_float).astype(jnp.bfloat16))
    gate_act = jnp.dot(mlp_in, gate_cols, preferred_element_type=jnp.float32)
    up_act = jnp.dot(mlp_in, up_cols, preferred_element_type=jnp.float32)
    hidden = (jax.nn.silu(gate_act) * up_act).astype(jnp.bfloat16)
    mlp_share = col_sums(jnp.dot(hidden, down_rows, preferred_element_type=jnp.float32))
    layer_output = (residual + mlp_share).astype(jnp.bfloat16)
    grad_float = grad_output.astype(jnp.float32)
    grad_full = widen(grad_output)
    grad_down = jnp.einsum("tf,td->fd", hidden, grad_full, preferred_element_type=jnp.float32)
    grad_hidden = jnp.einsum("td,fd->tf", grad_full, down_rows, preferred_element_type=jnp.float32)
    gate_sigmoid = jax.nn.sigmoid(gate_act)
    grad_gate_act = (
        grad_hidden * up_act * gate_sigmoid * (1.0 + gate_act * (1.0 - gate_sigmoid))
    ).astype(jnp.bfloat16)
    grad_up_act = (grad_hidden * gate_act * gate_sigmoid).astype(jnp.bfloat16)
    grad_gate = jnp.einsum("td,tf->df", mlp_in, grad_gate_act, preferred_element_type=jnp.float32)
    grad_up = jnp.einsum("td,tf->df", mlp_in, grad_up_act, preferred_element_type=jnp.float32)
    grad_mlp_share = col_sums(
        jnp.einsum("tf,df->td", grad_gate_act, gate_cols, preferred_element_type=jnp.float32)
        + jnp.einsum("tf,df->td", grad_up_act, up_cols, preferred_element_type=jnp.float32)
    )
    scaled_two = grad_mlp_share * mlp_gain_float
    inner_two = jnp.mean(scaled_two * normed_two, axis=1, keepdims=True)
    grad_residual = grad_float + inv_two * (scaled_two - normed_two * inner_two)
    grad_mlp_gain = jnp.sum(grad_mlp_share * normed_two, axis=0)
    grad_branch = grad_residual.astype(jnp.bfloat16)
    grad_attn_full = widen(grad_branch)
    grad_out_weight = jnp.einsum(
        "tq,td->qd", attn_tokens, grad_attn_full, preferred_element_type=jnp.float32
    )
    grad_mixture = to_rows(
        jnp.einsum(
            "td,qd->tq", grad_attn_full, out_rows, preferred_element_type=jnp.float32
        ).astype(jnp.bfloat16)
    )

    def back_block(carried_state, scan_items):
        block_index, block_log_total = scan_items
        first_row, allowed = block_inputs(block_index)

        def backward_head_group(inner_acc, group_items):
            group_index, log_group = group_items
            keys_acc, values_acc = inner_acc
            query_head_rows, key_group, value_group, scores = group_scores(
                query_rotated, group_index, allowed
            )
            attn_probs = jnp.exp(scores - log_group[:, :, None])
            grad_heads = lax.dynamic_slice_in_dim(
                grad_mixture, group_index * group_head_width, group_head_width, 1
            ).reshape(block_rows, heads_per_group, HEAD_SIZE_DIM)
            grad_probs = jnp.einsum(
                "qhd,kd->hqk", grad_heads, value_group, preferred_element_type=jnp.float32
            )
            value_piece = jnp.einsum(
                "hqk,qhd->kd",
                attn_probs.astype(jnp.bfloat16),
                grad_heads,
                preferred_element_type=jnp.float32,
            )
            inner_dot = jnp.sum(attn_probs * grad_probs, axis=2, keepdims=True)
            grad_scores = (attn_probs * (grad_probs - inner_dot)).astype(jnp.bfloat16)
            query_piece = jnp.einsum(
                "hqk,kd->qhd", grad_scores, key_group, preferred_element_type=jnp.float32
            ).reshape(block_rows, group_head_width)
            key_piece = jnp.einsum(
                "hqk,qhd->kd", grad_scores, query_head_rows, preferred_element_type=jnp.float32
            )
            column = group_index * HEAD_SIZE_DIM
            keys_acc = lax.dynamic_update_slice_in_dim(
                keys_acc,
                lax.dynamic_slice_in_dim(keys_acc, column, HEAD_SIZE_DIM, 1) + key_piece,
                column,
                1,
            )
            values_acc = lax.dynamic_update_slice_in_dim(
                values_acc,
                lax.dynamic_slice_in_dim(values_acc, column, HEAD_SIZE_DIM, 1) + value_piece,
                column,
                1,
            )
            return ((keys_acc, values_acc), query_piece)

        carried_state, query_pieces = lax.scan(
            backward_head_group,
            carried_state,
            (jnp.arange(KEY_VALUE_HEADS, dtype=jnp.int32), block_log_total),
        )
        return (
            carried_state,
            jnp.transpose(query_pieces, (1, 0, 2)).reshape(block_rows, query_width),
        )

    zeros_kv = jnp.zeros((token_rows, key_all.shape[1]), jnp.float32)
    (grad_keys, grad_values), query_blocks = lax.scan(
        back_block, (zeros_kv, zeros_kv), (jnp.arange(block_count, dtype=jnp.int32), log_blocks)
    )
    grad_query_rot = query_blocks.reshape(query_rows, query_width)
    grad_query_raw = to_tokens(
        rotary_back(grad_query_rot * score_scale, query_cos, query_sin, HEAD_SIZE_DIM).astype(
            jnp.bfloat16
        )
    )
    grad_key_part = rotary_back(grad_keys, key_cos, key_sin, HEAD_SIZE_DIM)
    grad_key_sum, grad_value_sum = (
        lax.psum_scatter(grad_key_part, "col", scatter_dimension=1, tiled=True),
        lax.psum_scatter(grad_values, "col", scatter_dimension=1, tiled=True),
    )
    grad_key_raw = grad_key_sum.astype(jnp.bfloat16)
    grad_value_raw = grad_value_sum.astype(jnp.bfloat16)
    grad_query = jnp.einsum(
        "td,tq->dq", attn_in, grad_query_raw, preferred_element_type=jnp.float32
    )
    grad_key = jnp.einsum("td,tq->dq", attn_in, grad_key_raw, preferred_element_type=jnp.float32)
    grad_value = jnp.einsum(
        "td,tq->dq", attn_in, grad_value_raw, preferred_element_type=jnp.float32
    )
    grad_attn_share = col_sums(
        jnp.einsum("tq,dq->td", grad_query_raw, query_cols, preferred_element_type=jnp.float32)
        + jnp.einsum("tq,dq->td", grad_key_raw, key_cols, preferred_element_type=jnp.float32)
        + jnp.einsum("tq,dq->td", grad_value_raw, value_cols, preferred_element_type=jnp.float32)
    )
    own_float = layer_input.astype(jnp.float32)
    inv_one = lax.rsqrt(jnp.mean(own_float * own_float, axis=1, keepdims=True) + eps)
    normed_one = own_float * inv_one
    scaled_one = grad_attn_share * attn_gain_float
    inner_one = jnp.mean(scaled_one * normed_one, axis=1, keepdims=True)
    grad_input = (grad_residual + inv_one * (scaled_one - normed_one * inner_one)).astype(
        jnp.bfloat16
    )
    grad_attn_gain = jnp.sum(grad_attn_share * normed_one, axis=0)
    weight_sums = (
        lax.psum_scatter(grad_query, "row", scatter_dimension=0, tiled=True),
        lax.psum_scatter(grad_key, "row", scatter_dimension=0, tiled=True),
        lax.psum_scatter(grad_value, "row", scatter_dimension=0, tiled=True),
        lax.psum_scatter(grad_out_weight, "row", scatter_dimension=1, tiled=True),
        lax.psum_scatter(grad_gate, "row", scatter_dimension=0, tiled=True),
        lax.psum_scatter(grad_up, "row", scatter_dimension=0, tiled=True),
        lax.psum_scatter(grad_down, "row", scatter_dimension=1, tiled=True),
    )
    gain_sums = lax.psum((grad_attn_gain, grad_mlp_gain), ("row", "col"))
    return (
        layer_output,
        grad_input,
        gain_sums[0],
        gain_sums[1],
        weight_sums[0],
        weight_sums[1],
        weight_sums[2],
        weight_sums[3],
        weight_sums[4],
        weight_sums[5],
        weight_sums[6],
    )


def solution(mesh):
    in_specs = (
        P(("row", "col"), None),
        P(),
        P(),
        P("row", "col"),
        P("row", "col"),
        P("row", "col"),
        P("col", "row"),
        P("row", "col"),
        P("row", "col"),
        P("col", "row"),
        P("row"),
        P("row"),
        P(("row", "col"), None),
    )
    out_specs = (
        P(("row", "col"), None),
        P(("row", "col"), None),
        P(),
        P(),
        P("row", "col"),
        P("row", "col"),
        P("row", "col"),
        P("col", "row"),
        P("row", "col"),
        P("row", "col"),
        P("col", "row"),
    )
    return jax.shard_map(shards, mesh=mesh, in_specs=in_specs, out_specs=out_specs, check_vma=False)
```

profile of v0, /device:TPU:0, one launch (start us, length us, event | category | flops | bytes accessed | tf_op | source)
XLA Modules:
  0.0 1523.2 jit_solution(14034235379282888117)
XLA Ops:
  14.5 24.8 %all_gather.42 = bf16[1152,192]{1,0:T(8,128)(2,1)S(1)} all-gather(bf16[72,192]{1,0:T(8,128)(2,1)S(1)} %copy-done.33), channel_id=1, replica_groups=mesh['row'=16,'col'=2] {'row'}, dimensions={0}, use_global_device_ids=true | all-gather | bytes 470016 | tf_op jit(solution)/shard_map/all_gather | solution.py:93
  39.4 19.0 %all_gather.40 = bf16[1152,192]{1,0:T(8,128)(2,1)S(1)} all-gather(bf16[72,192]{1,0:T(8,128)(2,1)S(1)} %copy-done.34), channel_id=1, replica_groups=mesh['row'=16,'col'=2] {'row'}, dimensions={0}, use_global_device_ids=true | all-gather | bytes 470016 | tf_op jit(solution)/shard_map/all_gather | solution.py:94
  62.2 12.0 all_gather.43
  76.2 11.4 all_gather.41
  90.0 4.0 convolution_convert_fusion.1
  95.1 3.6 all-to-all-start
  99.4 7.6 fusion.73
  107.0 7.4 all-to-all-done
  115.5 11.3 fusion.64
  126.8 62.2 %while.50 = (s32[]{:T(128)}, bf16[6,512,192]{1,2,0:T(8,128)(2,1)S(1)}, f32[6,3,512]{2,1,0:T(4,128)}, s32[6]{0:T(128)S(1)}, bf16[1024,384]{0,1:T(8,128)(2,1)}, /*...) while((s32[]{:T(128)}, ...), condition=%wide.region_6.7_spmd.clone.clone, body=%wide.region_3.6_spmd.clone.sunk.clone | while | flops 418380288 | bytes 22477056 | solution.py:168
  189.0 17.3 %all_to_all.64 = bf16[512,2,576]{0,2,1:T(8,128)(2,1)S(1)} all-to-all(bf16[512,2,576]{0,2,1:T(8,128)(2,1)S(1)} %bitcast.276), channel_id=1, replica_groups=mesh['row'=16,'col'=2] {'col'}, dimensions={1} | all-to-all | bytes 2359296 | tf_op jit(solution)/shard_map/all_to_all | solution.py:53
  206.6 6.2 fusion.124
  214.1 56.8 %reduce-scatter.18.cloned.1.call-done = f32[512,1152]{1,0:T(8,128)} async-done(((f32[1024,1152]{1,0:T(8,128)}), f32[512,1152]{1,0:T(8,128)}) %reduce-scatter.18.cloned.1.call-update) | async-done | bytes 2359312 | tf_op jit(solution)/shard_map/reduce_scatter | solution.py:57
  277.9 42.6 %all-gather.20.cloned.1.call-done = bf16[1152,1536]{1,0:T(8,128)(2,1)} async-done(((bf16[72,1536]{1,0:T(8,128)(2,1)}), bf16[1152,1536]{1,0:T(8,128)(2,1)}) %all-gather.20.cloned.1.call-update) | async-done | bytes 3538960 | tf_op jit(solution)/shard_map/all_gather | solution.py:97
  320.5 37.1 %all-gather.16.cloned.1.call-done = bf16[1024,1152]{1,0:T(8,128)(2,1)} async-done(((bf16[512,1152]{1,0:T(8,128)(2,1)}), bf16[1024,1152]{1,0:T(8,128)(2,1)}) %all-gather.16.cloned.1.call-update) | async-done | bytes 2359312 | tf_op jit(solution)/shard_map/all_gather | solution.py:61
  357.6 9.6 fusion.126
  367.3 40.2 %all-gather.18.cloned.1.call-done = bf16[1152,1536]{1,0:T(8,128)(2,1)} async-done(((bf16[72,1536]{1,0:T(8,128)(2,1)}), bf16[1152,1536]{1,0:T(8,128)(2,1)}) %all-gather.18.cloned.1.call-update) | async-done | bytes 3538960 | tf_op jit(solution)/shard_map/all_gather | solution.py:96
  407.4 9.7 fusion.125
  417.1 27.0 %all-gather.24.cloned.1.call-done = bf16[1024,1152]{1,0:T(8,128)(2,1)} async-done(((bf16[512,1152]{1,0:T(8,128)(2,1)}), bf16[1024,1152]{1,0:T(8,128)(2,1)}) %all-gather.24.cloned.1.call-update) | async-done | bytes 2359312 | tf_op jit(solution)/shard_map/all_gather | solution.py:61
  444.1 49.8 %all-gather.22.cloned.1.call-done = bf16[1536,1152]{0,1:T(8,128)(2,1)} async-done(((bf16[1536,72]{0,1:T(8,128)(2,1)}), bf16[1536,1152]{0,1:T(8,128)(2,1)}) %all-gather.22.cloned.1.call-update) | async-done | bytes 3538960 | tf_op jit(solution)/shard_map/all_gather | solution.py:98
  493.9 12.5 multiply_convert_fusion
  506.4 4.3 fusion.128
  510.7 6.0 convolution_add_fusion.2
  516.8 59.1 %reduce-scatter.22.cloned.1.call-done = f32[512,1152]{1,0:T(8,128)} async-done(((f32[1024,1152]{1,0:T(8,128)}), f32[512,1152]{1,0:T(8,128)}) %reduce-scatter.22.cloned.1.call-update) | async-done | bytes 2359312 | tf_op jit(solution)/shard_map/reduce_scatter | solution.py:57
  575.9 3.0 multiply_reduce_fusion
  581.8 36.2 %all-gather.26.cloned.1.call-done = bf16[1024,1152]{1,0:T(8,128)(2,1)} async-done(((bf16[512,1152]{1,0:T(8,128)(2,1)}), bf16[1024,1152]{1,0:T(8,128)(2,1)}) %all-gather.26.cloned.1.call-update) | async-done | bytes 2359312 | tf_op jit(solution)/shard_map/all_gather | solution.py:61
  618.1 3.8 convolution_convert_fusion
  623.0 4.4 all-to-all-start.2
  627.7 15.1 all-to-all-done.2
  645.5 125.0 %while.51 = (s32[]{:T(128)}, f32[1024,384]{0,1:T(8,128)}, f32[1024,384]{0,1:T(8,128)}, f32[6,512,192]{1,2,0:T(8,128)}, s32[6]{0:T(128)S(1)}, /*index=5*/bf16[102...) while((s32[]{:T(128)}, f32[1024,384]{0,1:T(8,128)}, ...), condition=%wide.region_15.16_spmd.clone.clone, body=%wide.region_13.15_spmd.clone.sunk.clone | while | flops 1027209728 | bytes 55630144 | solution.py:265
  652.1 3.3 fusion.231
  672.9 3.3 fusion.231
  693.8 3.3 fusion.231
  714.6 3.3 fusion.231
  735.4 3.3 fusion.231
  756.3 3.3 fusion.231
  770.5 6.5 fusion.70
  778.4 6.8 fusion.74
  786.3 8.0 fusion.51
  796.7 8.7 subtract_convert_fusion
  805.4 18.5 %all_to_all.65 = bf16[512,2,576]{0,2,1:T(8,128)(2,1)S(1)} all-to-all(bf16[512,2,576]{0,2,1:T(8,128)(2,1)S(1)} %subtract_convert_fusion), channel_id=1, replica_groups=mesh['row'=16,'col'=2] {'col'}, dimensions={1} | all-to-all | bytes 2359296 | tf_op jit(solution)/shard_map/all_to_all | solution.py:53
  824.1 4.3 fusion.129
  828.4 5.7 convolution_add_fusion.1
  834.1 6.9 reduce-scatter.26.cloned.1.call-done
  841.0 5.6 convolution_add_fusion
  846.7 9.4 fusion.127
  857.7 7.7 fusion.133
  867.1 7.6 fusion.132
  874.7 7.9 fusion.131
  883.9 5.4 fusion.130
  891.0 3.2 fusion.77
  894.2 3.2 fusion.80
  897.6 4.0 fusion.111
  903.0 3.8 reduce-scatter.28.cloned.1.call-done
  909.8 40.1 %all-reduce.2 = (f32[1152]{0:T(1024)}, f32[1152]{0:T(1024)}) all-reduce(f32[1152]{0:T(1024)} %get-tuple-element.251, f32[1152]{0:T(1024)} %get-tuple-element.249), channel_id=1, replica_groups=mesh['row'=16,'col'=2] {'row','col'}, use_global_device_ids=true, to_apply=%region_21.22 | all-reduce | flops 2304 | bytes 18432 | tf_op jit(solution)/shard_map/psum | solution.py:322
  951.1 19.2 %reduce-scatter.20.cloned.1.call-done = f32[512,1152]{1,0:T(8,128)} async-done(((f32[1024,1152]{1,0:T(8,128)}), f32[512,1152]{1,0:T(8,128)}) %reduce-scatter.20.cloned.1.call-update) | async-done | bytes 2359312 | tf_op jit(solution)/shard_map/reduce_scatter | solution.py:57
  970.3 5.1 fusion.60
  975.4 89.2 %reduce-scatter.38.cloned.1.call-done = f32[1536,72]{0,1:T(8,128)} async-done(((f32[1536,1152]{0,1:T(8,128)}), f32[1536,72]{0,1:T(8,128)}) %reduce-scatter.38.cloned.1.call-update) | async-done | bytes 442384 | tf_op jit(solution)/shard_map/reduce_scatter | solution.py:320
  1064.7 94.5 %reduce-scatter.36.cloned.1.call-done = f32[72,1536]{1,0:T(8,128)} async-done(((f32[1152,1536]{1,0:T(8,128)}), f32[72,1536]{1,0:T(8,128)}) %reduce-scatter.36.cloned.1.call-update) | async-done | bytes 442384 | tf_op jit(solution)/shard_map/reduce_scatter | solution.py:319
  1159.2 94.0 %reduce-scatter.34.cloned.1.call-done = f32[72,1536]{1,0:T(8,128)} async-done(((f32[1152,1536]{1,0:T(8,128)}), f32[72,1536]{1,0:T(8,128)}) %reduce-scatter.34.cloned.1.call-update) | async-done | bytes 442384 | tf_op jit(solution)/shard_map/reduce_scatter | solution.py:318
  1253.3 69.9 %reduce-scatter.42.cloned.1.call-done = f32[576,72]{0,1:T(8,128)} async-done(((f32[576,1152]{0,1:T(8,128)}), f32[576,72]{0,1:T(8,128)}) %reduce-scatter.42.cloned.1.call-update) | async-done | bytes 165904
  1323.1 61.6 %reduce-scatter.32.cloned.1.call-done = f32[72,192]{1,0:T(8,128)} async-done(((f32[1152,192]{1,0:T(8,128)}), f32[72,192]{1,0:T(8,128)}) %reduce-scatter.32.cloned.1.call-update) | async-done | bytes 55312 | tf_op jit(solution)/shard_map/reduce_scatter | solution.py:316
  1384.8 61.8 %reduce-scatter.30.cloned.1.call-done = f32[72,192]{1,0:T(8,128)} async-done(((f32[1152,192]{1,0:T(8,128)}), f32[72,192]{1,0:T(8,128)}) %reduce-scatter.30.cloned.1.call-update) | async-done | bytes 55312 | tf_op jit(solution)/shard_map/reduce_scatter | solution.py:315
  1446.6 69.3 %reduce-scatter.40.cloned.1.call-done = f32[72,576]{1,0:T(8,128)} async-done(((f32[1152,576]{1,0:T(8,128)}), f32[72,576]{1,0:T(8,128)}) %reduce-scatter.40.cloned.1.call-update) | async-done | bytes 165904
  (326 shorter events, 201.1 us)
Async XLA Ops:
  7.2 4.7 copy-start.19
  7.2 5.3 copy-start.20
  7.2 7.3 copy-start.41
  7.2 7.3 copy-start.33
  7.2 32.2 %copy-start.34 = (bf16[72,192]{1,0:T(8,128)(2,1)S(1)}, bf16[72,192]{1,0:T(8,128)(2,1)}, u32[]{:S(2)}) copy-start(bf16[72,192]{1,0:T(8,128)(2,1)} %param.22) | copy-start | bytes 82948
  7.2 51.2 %all-gather.10.cloned.1.call-start = ((), (), s32[]{:S(2)}) async-start(), calls=%async_computation.17 | async-start | bytes 3538944 | tf_op jit(solution)/shard_map/all_gather | solution.py:89
  8.0 82.0 %all-gather.12.cloned.1.call-start = ((), (), s32[]{:S(2)}) async-start(), calls=%async_computation.18 | async-start | bytes 1566720 | tf_op jit(solution)/shard_map/all_gather | solution.py:92
  8.7 197.8 %all-gather.14.cloned.1.call-start = ((), (), s32[]{:S(2)}) async-start(), calls=%async_computation.19 | async-start | bytes 1566720 | tf_op jit(solution)/shard_map/all_gather | solution.py:95
  13.9 47.0 %copy-start.24 = (f32[1024]{0:T(1024)}, f32[1024]{0:T(1024)S(1)}, u32[]{:S(2)}) copy-start(f32[1024]{0:T(1024)S(1)} %fusion.97) | copy-start | bytes 12292
  14.5 46.4 %copy-start.27 = (f32[1152]{0:T(1024)}, f32[1152]{0:T(1024)S(1)}, u32[]{:S(2)}) copy-start(f32[1152]{0:T(1024)S(1)} %convert_element_type.125) | copy-start | bytes 13828
  39.4 22.8 %copy-start.15 = (bf16[1152,192]{1,0:T(8,128)(2,1)}, bf16[1152,192]{1,0:T(8,128)(2,1)S(1)}, u32[]{:S(2)}) copy-start(bf16[1152,192]{1,0:T(8,128)(2,1)S(1)} %all_gather.42) | copy-start | bytes 1327108
  58.4 15.9 %copy-start.13 = (bf16[1152,192]{1,0:T(8,128)(2,1)}, bf16[1152,192]{1,0:T(8,128)(2,1)S(1)}, u32[]{:S(2)}) copy-start(bf16[1152,192]{1,0:T(8,128)(2,1)S(1)} %all_gather.40) | copy-start | bytes 1327108
  58.4 2.6 copy-start.10
  61.0 13.3 copy-start.43
  74.3 15.7 %copy-start.28 = (f32[1152]{0:T(1024)S(1)}, f32[1152]{0:T(1024)}, u32[]{:S(2)}) copy-start(f32[1152]{0:T(1024)} %copy-done.27) | copy-start | bytes 13828
  95.1 19.3 %all-to-all-start = ((bf16[2,512,576]{1,2,0:T(8,128)(2,1)}), bf16[2,512,576]{1,2,0:T(8,128)(2,1)S(1)}, u32[]{:S(2)}, u32[]{:S(2)}) async-start(bf16[2,512,576]{1,2,0:T(8,128)(2,1)} %bitcast.277), calls=%async_computation | async-start | bytes 2359296 | tf_op jit(solution)/shard_map/all_to_all | solution.py:49
  98.7 172.2 %reduce-scatter.18.cloned.1.call-start = ((), (), s32[]{:S(2)}) async-start(), calls=%async_computation.20 | async-start | bytes 7077888 | tf_op jit(solution)/shard_map/reduce_scatter | solution.py:57
  206.5 6.3 copy-start.17
  212.8 58.1 %copy-start.7 = (bf16[512,1152]{1,0:T(8,128)(2,1)S(1)}, bf16[512,1152]{1,0:T(8,128)(2,1)}, u32[]{:S(2)}) copy-start(bf16[512,1152]{1,0:T(8,128)(2,1)} %param.17) | copy-start | bytes 3538948
  212.8 107.7 %all-gather.20.cloned.1.call-start = ((), (), s32[]{:S(2)}) async-start(), calls=%async_computation.23 | async-start | bytes 3760128 | tf_op jit(solution)/shard_map/all_gather | solution.py:97
  213.4 144.2 %all-gather.16.cloned.1.call-start = ((), (), s32[]{:S(2)}) async-start(), calls=%async_computation.21 | async-start | bytes 3538944 | tf_op jit(solution)/shard_map/all_gather | solution.py:61
  270.9 2.8 copy-start.21
  273.7 305.2 %copy-start.1 = (f32[512,1152]{1,0:T(8,128)}, f32[512,1152]{1,0:T(8,128)S(1)}, u32[]{:S(2)}) copy-start(f32[512,1152]{1,0:T(8,128)S(1)} %get-tuple-element.306) | copy-start | bytes 7077892
  275.3 132.2 %all-gather.18.cloned.1.call-start = ((), (), s32[]{:S(2)}) async-start(), calls=%async_computation.22 | async-start | bytes 3760128 | tf_op jit(solution)/shard_map/all_gather | solution.py:96
  276.0 168.1 %all-gather.24.cloned.1.call-start = ((), (), s32[]{:S(2)}) async-start(), calls=%async_computation.26 | async-start | bytes 3538944 | tf_op jit(solution)/shard_map/all_gather | solution.py:61
  276.8 217.1 %all-gather.22.cloned.1.call-start = ((), (), s32[]{:S(2)}) async-start(), calls=%async_computation.24 | async-start | bytes 3760128 | tf_op jit(solution)/shard_map/all_gather | solution.py:98
  277.5 298.4 %reduce-scatter.22.cloned.1.call-start = ((), (), s32[]{:S(2)}) async-start(), calls=%async_computation.27 | async-start | bytes 7077888 | tf_op jit(solution)/shard_map/reduce_scatter | solution.py:57
  493.9 12.5 copy-start.48
  506.4 4.3 copy-start.52
  506.4 4.3 copy-start.53
  506.4 4.3 copy-start.47
  516.7 62.8 %copy-start.9 = (bf16[512,1152]{1,0:T(8,128)(2,1)S(1)}, bf16[512,1152]{1,0:T(8,128)(2,1)}, u32[]{:S(2)}) copy-start(bf16[512,1152]{1,0:T(8,128)(2,1)} %param.29) | copy-start | bytes 3538948
  516.7 101.3 %all-gather.26.cloned.1.call-start = ((), (), s32[]{:S(2)}) async-start(), calls=%async_computation.28 | async-start | bytes 3538944 | tf_op jit(solution)/shard_map/all_gather | solution.py:61
  575.9 3.6 copy-start.6
  575.9 3.6 copy-start.22
  623.0 19.8 %all-to-all-start.2 = ((bf16[2,512,576]{1,2,0:T(8,128)(2,1)}), bf16[2,512,576]{1,2,0:T(8,128)(2,1)}, u32[]{:S(2)}, u32[]{:S(2)}) async-start(bf16[2,512,576]{1,2,0:T(8,128)(2,1)} %bitcast.162), calls=%async_computation.5 | async-start | bytes 2359296 | tf_op jit(solution)/shard_map/all_to_all | solution.py:49
  627.4 201.0 %reduce-scatter.24.cloned.1.call-start = ((), (), s32[]{:S(2)}) async-start(), calls=%async_computation.29 | async-start | bytes 2359296 | tf_op jit(solution)/shard_map/reduce_scatter | solution.py:287
  645.5 125.0 %copy-start.26 = (f32[1024]{0:T(1024)S(1)}, f32[1024]{0:T(1024)}, u32[]{:S(2)}) copy-start(f32[1024]{0:T(1024)} %copy-done.24) | copy-start | bytes 12292
  645.5 125.0 %copy-start.36 = (f32[384]{0:T(512)S(1)}, f32[384]{0:T(512)}, u32[]{:S(2)}) copy-start(f32[384]{0:T(512)} %fusion.100) | copy-start | bytes 4612
  650.0 5.4 copy-start
  670.8 5.4 copy-start
  691.7 5.4 copy-start
  712.5 5.4 copy-start
  733.3 5.4 copy-start
  754.2 5.4 copy-start
  778.4 7.2 copy-start.12
  785.3 55.7 %reduce-scatter.26.cloned.1.call-start = ((), (), s32[]{:S(2)}) async-start(), calls=%async_computation.30 | async-start | bytes 2359296 | tf_op jit(solution)/shard_map/reduce_scatter | solution.py:288
  786.3 8.0 copy-start.4
  794.4 112.4 %reduce-scatter.28.cloned.1.call-start = ((), (), s32[]{:S(2)}) async-start(), calls=%async_computation.31 | async-start | bytes 7077888 | tf_op jit(solution)/shard_map/reduce_scatter | solution.py:57
  795.0 1.7 copy-start.5
  805.4 18.7 %copy-start.51 = (bf16[1152,576]{1,0:T(8,128)(2,1)S(1)}, bf16[1152,576]{1,0:T(8,128)(2,1)}, u32[]{:S(2)}) copy-start(bf16[1152,576]{1,0:T(8,128)(2,1)} %all-gather.12.cloned.1.call-done) | copy-start | bytes 3981316
  824.1 4.4 copy-start.16
  828.4 12.6 copy-start.14
  846.7 123.7 %reduce-scatter.20.cloned.1.call-start = ((), (), s32[]{:S(2)}) async-start(), calls=%async_computation.25 | async-start | bytes 7077888 | tf_op jit(solution)/shard_map/reduce_scatter | solution.py:57
  856.1 208.6 %reduce-scatter.38.cloned.1.call-start = ((), (), s32[]{:S(2)}) async-start(), calls=%async_computation.36 | async-start | bytes 7520256 | tf_op jit(solution)/shard_map/reduce_scatter | solution.py:320
  865.4 293.8 %reduce-scatter.36.cloned.1.call-start = ((), (), s32[]{:S(2)}) async-start(), calls=%async_computation.35 | async-start | bytes 7520256 | tf_op jit(solution)/shard_map/reduce_scatter | solution.py:319
  874.7 378.6 %reduce-scatter.34.cloned.1.call-start = ((), (), s32[]{:S(2)}) async-start(), calls=%async_computation.34 | async-start | bytes 7520256 | tf_op jit(solution)/shard_map/reduce_scatter | solution.py:318
  882.6 440.5 %reduce-scatter.42.cloned.1.call-start = ((), (), s32[]{:S(2)}) async-start(), calls=%async_computation.38 | async-start | bytes 3133440
  889.3 495.4 %reduce-scatter.32.cloned.1.call-start = ((), (), s32[]{:S(2)}) async-start(), calls=%async_computation.33 | async-start | bytes 1253376 | tf_op jit(solution)/shard_map/reduce_scatter | solution.py:316
  894.2 552.4 %reduce-scatter.30.cloned.1.call-start = ((), (), s32[]{:S(2)}) async-start(), calls=%async_computation.32 | async-start | bytes 1253376 | tf_op jit(solution)/shard_map/reduce_scatter | solution.py:315
  897.5 618.4 %reduce-scatter.40.cloned.1.call-start = ((), (), s32[]{:S(2)}) async-start(), calls=%async_computation.37 | async-start | bytes 3133440
  901.6 5.3 copy-start.8
  901.6 68.7 %copy-start.2 = (f32[512,1152]{1,0:T(8,128)S(1)}, f32[512,1152]{1,0:T(8,128)}, u32[]{:S(2)}) copy-start(f32[512,1152]{1,0:T(8,128)} %copy-done.1) | copy-start | bytes 7077892
  901.6 68.7 %copy-start.23 = (f32[1152]{0:T(1024)S(1)}, f32[1152]{0:T(1024)}, u32[]{:S(2)}) copy-start(f32[1152]{0:T(1024)} %convert_element_type.142) | copy-start | bytes 13828
  (19 other events, 20.9 us)
Sparse Core Ops, SparseCore 0:
  9.6 38.7 all-gather.9
  50.6 39.3 all-gather.11
  92.1 38.1 all-gather.13
  212.9 57.8 reduce-scatter.17
  273.3 47.1 all-gather.19
  322.5 35.0 all-gather.15
  360.2 47.1 all-gather.17
  409.0 35.0 all-gather.23
  446.7 47.1 all-gather.21
  516.8 58.9 reduce-scatter.21
  582.0 36.0 all-gather.25
  785.4 26.4 reduce-scatter.23
  814.2 26.7 reduce-scatter.25
  846.8 59.9 reduce-scatter.27
  909.1 61.2 reduce-scatter.19
  974.8 89.8 reduce-scatter.37
  1069.6 89.5 reduce-scatter.35
  1163.7 89.5 reduce-scatter.33
  1258.3 64.8 reduce-scatter.41
  1327.6 57.0 reduce-scatter.31
  1389.4 57.1 reduce-scatter.29
  1451.6 64.2 reduce-scatter.39
where the time goes:
time: 1530 us; the launch traced here: 1520 us
  waiting for transfers between devices  949 us (62%)
  matrix products  228 us (15%)
  blocking collectives  143 us (9%)
  other arithmetic  115 us (8%)
  local copies, waits for them, and re-layouts  45.7 us (3%)
  loops' own time  16.1 us (1%)
  between operations  16.1 us (1%)
    unnamed x24, waiting for transfers between devices  144 us
    reduce_scatter x4, waiting for transfers between devices, col_sums(): return lax.psum_scatter(values, 'col', scatter_dimension=0, tiled=True)  139 us
    all_gather x3, waiting for transfers between devices, widen(): return lax.all_gather(values, 'col', axis=0, tiled=True)  100 us
    reduce_scatter x1, waiting for transfers between devices, shards(): lax.psum_scatter(grad_up, 'row', scatter_dimension=0, tiled=True)  94.5 us
    reduce_scatter x1, waiting for transfers between devices, shards(): lax.psum_scatter(grad_gate, 'row', scatter_dimension=0, tiled=True)  94 us
    reduce_scatter x1, waiting for transfers between devices, shards(): lax.psum_scatter(grad_down, 'row', scatter_dimension=1, tiled=True)  89.2 us
    reduce_scatter x1, waiting for transfers between devices, shards(): lax.psum_scatter(grad_key, 'row', scatter_dimension=0, tiled=True)  61.8 us
    reduce_scatter x1, waiting for transfers between devices, shards(): lax.psum_scatter(grad_value, 'row', scatter_dimension=0, tiled=True)  61.6 us
  transfers between devices with their start and end apart: 24, of which 21 were waited for; matrix products, arithmetic and copies ran while one was open for 13% of the time, Pallas kernels for 0%

commit v1 on v0

--- a/solution.py
+++ b/solution.py
@@ -88,12 +88,39 @@
     mlp_gain_float = mlp_gain.astype(jnp.float32)
     full_input = lax.all_gather(layer_input, "col", axis=0, tiled=True)
     token_rows = full_input.shape[0]
+
+    def _attach_column(mine, net_axis, k_dim):
+        arr_now, spare, w2 = (
+            jax.lax.axis_size(net_axis),
+            jax.lax.axis_index(net_axis),
+            mine.shape[k_dim],
+        )
+        log = tuple(((pp, (pp + 1) % arr_now) for pp in range(arr_now)))
+        sides = tuple(((pp, (pp - 1) % arr_now) for pp in range(arr_now)))
+        u_next = jnp.zeros(
+            (*mine.shape[:k_dim], arr_now * w2, *mine.shape[k_dim + 1 :]), mine.dtype
+        )
+        u_next = lax.dynamic_update_slice_in_dim(u_next, mine, spare * w2, axis=k_dim)
+        h_now = outer = mine
+        front = arr_now // 2
+        for no in range(1, front + 1):
+            h_now = jax.lax.ppermute(h_now, axis_name=net_axis, perm=log)
+            u_next = lax.dynamic_update_slice_in_dim(
+                u_next, h_now, (spare - no) % arr_now * w2, axis=k_dim
+            )
+            if no < arr_now - front:
+                outer = jax.lax.ppermute(outer, net_axis, perm=sides)
+                u_next = lax.dynamic_update_slice_in_dim(
+                    u_next, outer, (spare + no) % arr_now * w2, axis=k_dim
+                )
+        return u_next
+
     query_cols, key_cols, value_cols, out_rows, gate_cols, up_cols, down_rows = (
         lax.all_gather(query_weight, "row", axis=0, tiled=True),
         lax.all_gather(key_weight, "row", axis=0, tiled=True),
         lax.all_gather(value_weight, "row", axis=0, tiled=True),
         lax.all_gather(out_weight, "row", axis=1, tiled=True),
-        lax.all_gather(gate_weight, "row", axis=0, tiled=True),
+        _attach_column(gate_weight, "row", 0),
         lax.all_gather(up_weight, "row", axis=0, tiled=True),
         lax.all_gather(down_weight, "row", axis=1, tiled=True),
     )

time: 1530 us -> 1490 us (0.974)
  waiting for transfers between devices: 949 us -> 864 us
  starting transfers between devices: 10.2 us -> 38.1 us
  local copies, waits for them, and re-layouts: 45.7 us -> 62.8 us
    reduce_scatter x4, waiting for transfers between devices: 139 us -> 97.5 us  [col_sums(): return lax.psum_scatter(values, 'col', scatter_dimension=0, tiled=True)]
    all_gather x1 -> x0, waiting for transfers between devices: 40.2 us -> none  [shards(): lax.all_gather(gate_weight, 'row', axis=0, tiled=True)]
    ppermute x0 -> x15, starting transfers between devices: none -> 27.9 us  [the longest x7 27.5 us: _attach_column(): outer = jax.lax.ppermute(outer, net_axis, perm=sides)]
    ppermute x0 -> x15, waiting for transfers between devices: none -> 19.8 us  [the longest x8 11.7 us: _attach_column(): h_now = jax.lax.ppermute(h_now, axis_name=net_axis, perm=log)]
    all_gather x3, waiting for transfers between devices: 100 us -> 82.2 us  [widen(): return lax.all_gather(values, 'col', axis=0, tiled=True)]
    unnamed x24 -> x23, waiting for transfers between devices: 144 us -> 143 us
  transfers between devices with their start and end apart: 24 -> 38, of which waited for: 21 -> 27; matrix products, arithmetic and copies ran while one was open for 13% -> 14% of each run, Pallas kernels for 0% -> 0%
where the time goes in v1:
time: 1490 us; the launch traced here: 1480 us
  waiting for transfers between devices  864 us (58%)
  matrix products  229 us (15%)
  blocking collectives  143 us (10%)
  other arithmetic  116 us (8%)
  local copies, waits for them, and re-layouts  62.8 us (4%)
  starting transfers between devices  38.1 us (3%)
  loops' own time  16.1 us (1%)
  between operations  15.9 us (1%)
    unnamed x23, waiting for transfers between devices  143 us
    reduce_scatter x4, waiting for transfers between devices, col_sums(): return lax.psum_scatter(values, 'col', scatter_dimension=0, tiled=True)  97.5 us
    reduce_scatter x1, waiting for transfers between devices, shards(): lax.psum_scatter(grad_gate, 'row', scatter_dimension=0, tiled=True)  94.5 us
    reduce_scatter x1, waiting for transfers between devices, shards(): lax.psum_scatter(grad_up, 'row', scatter_dimension=0, tiled=True)  94.1 us
    reduce_scatter x1, waiting for transfers between devices, shards(): lax.psum_scatter(grad_down, 'row', scatter_dimension=1, tiled=True)  89.2 us
    all_gather x3, waiting for transfers between devices, widen(): return lax.all_gather(values, 'col', axis=0, tiled=True)  82.2 us
    reduce_scatter x1, waiting for transfers between devices, shards(): lax.psum_scatter(grad_value, 'row', scatter_dimension=0, tiled=True)  61.8 us
    reduce_scatter x1, waiting for transfers between devices, shards(): lax.psum_scatter(grad_key, 'row', scatter_dimension=0, tiled=True)  61.6 us
  transfers between devices with their start and end apart: 38, of which 27 were waited for; matrix products, arithmetic and copies ran while one was open for 14% of the time, Pallas kernels for 0%

profile of v1, /device:TPU:0, one launch (start us, length us, event | category | flops | bytes accessed | tf_op | source)
XLA Modules:
  0.0 1484.5 jit_solution(16781749283613685557)
XLA Ops:
  14.6 24.8 %all_gather.39 = bf16[1152,192]{1,0:T(8,128)(2,1)S(1)} all-gather(bf16[72,192]{1,0:T(8,128)(2,1)S(1)} %copy-done.33), channel_id=1, replica_groups=mesh['row'=16,'col'=2] {'row'}, dimensions={0}, use_global_device_ids=true | all-gather | bytes 470016 | tf_op jit(solution)/shard_map/all_gather | solution.py:120
  39.4 19.0 %all_gather.37 = bf16[1152,192]{1,0:T(8,128)(2,1)S(1)} all-gather(bf16[72,192]{1,0:T(8,128)(2,1)S(1)} %copy-done.34), channel_id=1, replica_groups=mesh['row'=16,'col'=2] {'row'}, dimensions={0}, use_global_device_ids=true | all-gather | bytes 470016 | tf_op jit(solution)/shard_map/all_gather | solution.py:121
  62.3 12.0 all_gather.40
  76.3 11.4 all_gather.38
  89.9 4.0 convolution_convert_fusion.1
  95.1 3.6 all-to-all-start
  99.6 7.6 fusion.73
  107.2 7.1 all-to-all-done
  115.5 11.3 fusion.64
  126.8 62.2 %while.50 = (s32[]{:T(128)}, bf16[6,512,192]{1,2,0:T(8,128)(2,1)S(1)}, f32[6,3,512]{2,1,0:T(4,128)}, s32[6]{0:T(128)S(1)}, bf16[1024,384]{0,1:T(8,128)(2,1)}, /*...) while((s32[]{:T(128)}, ...), condition=%wide.region_6.7_spmd.clone.clone, body=%wide.region_3.6_spmd.clone.sunk.clone | while | flops 418380288 | bytes 22477056 | solution.py:195
  189.0 17.3 %all_to_all.64 = bf16[512,2,576]{0,2,1:T(8,128)(2,1)S(1)} all-to-all(bf16[512,2,576]{0,2,1:T(8,128)(2,1)S(1)} %bitcast.276), channel_id=1, replica_groups=mesh['row'=16,'col'=2] {'col'}, dimensions={1} | all-to-all | bytes 2359296 | tf_op jit(solution)/shard_map/all_to_all | solution.py:53
  206.6 6.2 fusion.124
  218.6 4.6 collective-permute-start.3
  226.6 4.7 collective-permute-start.5
  234.8 4.7 collective-permute-start.7
  243.0 4.7 collective-permute-start.9
  251.1 4.8 collective-permute-start.11
  256.1 14.7 reduce-scatter.18.cloned.1.call-done
  279.0 3.7 collective-permute-start.13
  286.0 5.0 collective-permute-done.12
  292.4 6.6 collective-permute-done.14
  299.7 8.7 all-gather.21.cloned.1.call-done
  308.4 49.6 %all-gather.19.cloned.1.call-done = bf16[1536,1152]{0,1:T(8,128)(2,1)} async-done(((bf16[1536,72]{0,1:T(8,128)(2,1)}), bf16[1536,1152]{0,1:T(8,128)(2,1)}) %all-gather.19.cloned.1.call-update) | async-done | bytes 3538960 | tf_op jit(solution)/shard_map/all_gather | solution.py:125
  358.0 9.7 fusion.127
  367.7 39.1 %all-gather.17.cloned.1.call-done = bf16[1152,1536]{1,0:T(8,128)(2,1)} async-done(((bf16[72,1536]{1,0:T(8,128)(2,1)}), bf16[1152,1536]{1,0:T(8,128)(2,1)}) %all-gather.17.cloned.1.call-update) | async-done | bytes 3538960 | tf_op jit(solution)/shard_map/all_gather | solution.py:124
  406.8 37.3 %all-gather.15.cloned.1.call-done = bf16[1024,1152]{1,0:T(8,128)(2,1)} async-done(((bf16[512,1152]{1,0:T(8,128)(2,1)}), bf16[1024,1152]{1,0:T(8,128)(2,1)}) %all-gather.15.cloned.1.call-update) | async-done | bytes 2359312 | tf_op jit(solution)/shard_map/all_gather | solution.py:61
  444.1 9.7 fusion.125
  453.8 11.2 multiply_convert_fusion.1
  465.0 4.2 fusion.128
  469.3 8.0 convolution_add_fusion.2
  477.8 59.7 %reduce-scatter.22.cloned.1.call-done = f32[512,1152]{1,0:T(8,128)} async-done(((f32[1024,1152]{1,0:T(8,128)}), f32[512,1152]{1,0:T(8,128)}) %reduce-scatter.22.cloned.1.call-update) | async-done | bytes 2359312 | tf_op jit(solution)/shard_map/reduce_scatter | solution.py:57
  543.5 36.2 %all-gather.23.cloned.1.call-done = bf16[1024,1152]{1,0:T(8,128)(2,1)} async-done(((bf16[512,1152]{1,0:T(8,128)(2,1)}), bf16[1024,1152]{1,0:T(8,128)(2,1)}) %all-gather.23.cloned.1.call-update) | async-done | bytes 2359312 | tf_op jit(solution)/shard_map/all_gather | solution.py:61
  579.7 3.8 convolution_convert_fusion
  584.6 4.5 all-to-all-start.2
  589.1 15.3 %all-to-all-done.2 = bf16[2,512,576]{1,2,0:T(8,128)(2,1)} async-done(((bf16[2,512,576]{1,2,0:T(8,128)(2,1)}), bf16[2,512,576]{1,2,0:T(8,128)(2,1)}, u32[]{:S(2)}, u32[]{:S(2)}) %all-to-all-start.2) | async-done | bytes 1179680 | tf_op jit(solution)/shard_map/all_to_all | solution.py:49
  607.2 125.1 %while.51 = (s32[]{:T(128)}, f32[1024,384]{0,1:T(8,128)}, f32[1024,384]{0,1:T(8,128)}, f32[6,512,192]{1,2,0:T(8,128)}, s32[6]{0:T(128)S(1)}, /*index=5*/bf16[102...) while((s32[]{:T(128)}, f32[1024,384]{0,1:T(8,128)}, ...), condition=%wide.region_15.16_spmd.clone.clone, body=%wide.region_13.15_spmd.clone.sunk.clone | while | flops 1027209728 | bytes 55630144 | solution.py:292
  634.6 3.4 fusion.231
  697.2 3.3 fusion.231
  732.3 6.5 fusion.70
  740.2 6.8 fusion.74
  748.0 8.0 fusion.51
  758.4 8.7 subtract_convert_fusion
  767.1 18.8 %all_to_all.65 = bf16[512,2,576]{0,2,1:T(8,128)(2,1)S(1)} all-to-all(bf16[512,2,576]{0,2,1:T(8,128)(2,1)S(1)} %subtract_convert_fusion), channel_id=1, replica_groups=mesh['row'=16,'col'=2] {'col'}, dimensions={1} | all-to-all | bytes 2359296 | tf_op jit(solution)/shard_map/all_to_all | solution.py:53
  786.1 4.4 fusion.129
  790.5 5.8 convolution_add_fusion.1
  796.3 6.5 reduce-scatter.26.cloned.1.call-done
  802.8 5.7 convolution_add_fusion
  808.6 9.4 fusion.126
  819.6 7.6 fusion.133
  828.9 7.6 fusion.131
  836.6 7.9 fusion.132
  845.7 5.3 fusion.130
  859.3 4.0 fusion.111
  864.7 4.0 reduce-scatter.28.cloned.1.call-done
  871.6 40.1 %all-reduce.2 = (f32[1152]{0:T(1024)}, f32[1152]{0:T(1024)}) all-reduce(f32[1152]{0:T(1024)} %get-tuple-element.251, f32[1152]{0:T(1024)} %get-tuple-element.249), channel_id=1, replica_groups=mesh['row'=16,'col'=2] {'row','col'}, use_global_device_ids=true, to_apply=%region_21.22 | all-reduce | flops 2304 | bytes 18432 | tf_op jit(solution)/shard_map/psum | solution.py:349
  913.0 19.2 %reduce-scatter.20.cloned.1.call-done = f32[512,1152]{1,0:T(8,128)} async-done(((f32[1024,1152]{1,0:T(8,128)}), f32[512,1152]{1,0:T(8,128)}) %reduce-scatter.20.cloned.1.call-update) | async-done | bytes 2359312 | tf_op jit(solution)/shard_map/reduce_scatter | solution.py:57
  932.2 5.1 fusion.60
  937.3 89.2 %reduce-scatter.38.cloned.1.call-done = f32[1536,72]{0,1:T(8,128)} async-done(((f32[1536,1152]{0,1:T(8,128)}), f32[1536,72]{0,1:T(8,128)}) %reduce-scatter.38.cloned.1.call-update) | async-done | bytes 442384 | tf_op jit(solution)/shard_map/reduce_scatter | solution.py:347
  1026.5 94.5 %reduce-scatter.34.cloned.1.call-done = f32[72,1536]{1,0:T(8,128)} async-done(((f32[1152,1536]{1,0:T(8,128)}), f32[72,1536]{1,0:T(8,128)}) %reduce-scatter.34.cloned.1.call-update) | async-done | bytes 442384 | tf_op jit(solution)/shard_map/reduce_scatter | solution.py:345
  1121.0 94.1 %reduce-scatter.36.cloned.1.call-done = f32[72,1536]{1,0:T(8,128)} async-done(((f32[1152,1536]{1,0:T(8,128)}), f32[72,1536]{1,0:T(8,128)}) %reduce-scatter.36.cloned.1.call-update) | async-done | bytes 442384 | tf_op jit(solution)/shard_map/reduce_scatter | solution.py:346
  1215.2 69.6 %reduce-scatter.42.cloned.1.call-done = f32[576,72]{0,1:T(8,128)} async-done(((f32[576,1152]{0,1:T(8,128)}), f32[576,72]{0,1:T(8,128)}) %reduce-scatter.42.cloned.1.call-update) | async-done | bytes 165904
  1284.8 61.8 %reduce-scatter.32.cloned.1.call-done = f32[72,192]{1,0:T(8,128)} async-done(((f32[1152,192]{1,0:T(8,128)}), f32[72,192]{1,0:T(8,128)}) %reduce-scatter.32.cloned.1.call-update) | async-done | bytes 55312 | tf_op jit(solution)/shard_map/reduce_scatter | solution.py:343
  1346.6 61.6 %reduce-scatter.30.cloned.1.call-done = f32[72,192]{1,0:T(8,128)} async-done(((f32[1152,192]{1,0:T(8,128)}), f32[72,192]{1,0:T(8,128)}) %reduce-scatter.30.cloned.1.call-update) | async-done | bytes 55312 | tf_op jit(solution)/shard_map/reduce_scatter | solution.py:342
  1408.2 69.3 %reduce-scatter.40.cloned.1.call-done = f32[72,576]{1,0:T(8,128)} async-done(((f32[1152,576]{1,0:T(8,128)}), f32[72,576]{1,0:T(8,128)}) %reduce-scatter.40.cloned.1.call-update) | async-done | bytes 165904
  (372 shorter events, 249.4 us)
Async XLA Ops:
  7.2 7.4 copy-start.41
  7.2 7.4 copy-start.33
  7.2 32.2 %copy-start.34 = (bf16[72,192]{1,0:T(8,128)(2,1)S(1)}, bf16[72,192]{1,0:T(8,128)(2,1)}, u32[]{:S(2)}) copy-start(bf16[72,192]{1,0:T(8,128)(2,1)} %param.22) | copy-start | bytes 82948
  7.2 51.2 %all-gather.9.cloned.1.call-start = ((), (), s32[]{:S(2)}) async-start(), calls=%async_computation.17 | async-start | bytes 3538944 | tf_op jit(solution)/shard_map/all_gather | solution.py:89
  8.0 82.0 %all-gather.11.cloned.1.call-start = ((), (), s32[]{:S(2)}) async-start(), calls=%async_computation.18 | async-start | bytes 1566720 | tf_op jit(solution)/shard_map/all_gather | solution.py:119
  8.7 197.8 %all-gather.13.cloned.1.call-start = ((), (), s32[]{:S(2)}) async-start(), calls=%async_computation.19 | async-start | bytes 1566720 | tf_op jit(solution)/shard_map/all_gather | solution.py:122
  13.9 47.0 %copy-start.24 = (f32[1024]{0:T(1024)}, f32[1024]{0:T(1024)S(1)}, u32[]{:S(2)}) copy-start(f32[1024]{0:T(1024)S(1)} %fusion.97) | copy-start | bytes 12292
  14.6 46.4 %copy-start.27 = (f32[1152]{0:T(1024)}, f32[1152]{0:T(1024)S(1)}, u32[]{:S(2)}) copy-start(f32[1152]{0:T(1024)S(1)} %convert_element_type.125) | copy-start | bytes 13828
  39.4 22.8 %copy-start.15 = (bf16[1152,192]{1,0:T(8,128)(2,1)}, bf16[1152,192]{1,0:T(8,128)(2,1)S(1)}, u32[]{:S(2)}) copy-start(bf16[1152,192]{1,0:T(8,128)(2,1)S(1)} %all_gather.39) | copy-start | bytes 1327108
  58.5 15.9 %copy-start.13 = (bf16[1152,192]{1,0:T(8,128)(2,1)}, bf16[1152,192]{1,0:T(8,128)(2,1)S(1)}, u32[]{:S(2)}) copy-start(bf16[1152,192]{1,0:T(8,128)(2,1)S(1)} %all_gather.37) | copy-start | bytes 1327108
  61.1 13.3 copy-start.43
  74.3 15.6 %copy-start.28 = (f32[1152]{0:T(1024)S(1)}, f32[1152]{0:T(1024)}, u32[]{:S(2)}) copy-start(f32[1152]{0:T(1024)} %copy-done.27) | copy-start | bytes 13828
  95.1 19.3 %all-to-all-start = ((bf16[2,512,576]{1,2,0:T(8,128)(2,1)}), bf16[2,512,576]{1,2,0:T(8,128)(2,1)S(1)}, u32[]{:S(2)}, u32[]{:S(2)}) async-start(bf16[2,512,576]{1,2,0:T(8,128)(2,1)} %bitcast.277), calls=%async_computation | async-start | bytes 2359296 | tf_op jit(solution)/shard_map/all_to_all | solution.py:49
  98.7 172.1 %reduce-scatter.18.cloned.1.call-start = ((), (), s32[]{:S(2)}) async-start(), calls=%async_computation.20 | async-start | bytes 7077888 | tf_op jit(solution)/shard_map/reduce_scatter | solution.py:57
  206.5 6.2 copy-start.17
  212.8 95.6 %all-gather.21.cloned.1.call-start = ((), (), s32[]{:S(2)}) async-start(), calls=%async_computation.25 | async-start | bytes 3538944 | tf_op jit(solution)/shard_map/all_gather | solution.py:61
  213.3 144.7 %all-gather.19.cloned.1.call-start = ((), (), s32[]{:S(2)}) async-start(), calls=%async_computation.23 | async-start | bytes 3760128 | tf_op jit(solution)/shard_map/all_gather | solution.py:125
  213.9 192.9 %all-gather.17.cloned.1.call-start = ((), (), s32[]{:S(2)}) async-start(), calls=%async_computation.22 | async-start | bytes 3760128 | tf_op jit(solution)/shard_map/all_gather | solution.py:124
  214.7 229.4 %all-gather.15.cloned.1.call-start = ((), (), s32[]{:S(2)}) async-start(), calls=%async_computation.21 | async-start | bytes 3538944 | tf_op jit(solution)/shard_map/all_gather | solution.py:61
  214.7 3.9 collective-permute-start.1
  215.0 8.2 collective-permute-start
  217.9 52.9 %copy-start.7 = (bf16[512,1152]{1,0:T(8,128)(2,1)S(1)}, bf16[512,1152]{1,0:T(8,128)(2,1)}, u32[]{:S(2)}) copy-start(bf16[512,1152]{1,0:T(8,128)(2,1)} %param.17) | copy-start | bytes 3538948
  218.6 8.1 collective-permute-start.3
  223.2 8.2 collective-permute-start.2
  226.6 8.2 collective-permute-start.5
  231.4 8.2 collective-permute-start.4
  234.8 8.2 collective-permute-start.7
  239.5 8.2 collective-permute-start.6
  243.0 8.2 collective-permute-start.9
  247.7 8.3 collective-permute-start.8
  251.1 27.9 %collective-permute-start.11 = (bf16[72,1536]{1,0:T(8,128)(2,1)}, bf16[72,1536]{1,0:T(8,128)(2,1)}, u32[]{:S(2)}, u32[]{:S(2)}) collective-permute-start(bf16[72,1536]{1,0:T(8,128)(2,1)} %collective-permute-done.9), channel_id=1, source_target_pairs={{0,30},{2,0},{4,2},{6,4},{8,6},{10,8},{12,10},{14,12},{16,14},{18,... | collective-permute-start | bytes 663560 | tf_op jit(solution)/shard_map/ppermute | solution.py:112
  256.0 26.7 %collective-permute-start.10 = (bf16[72,1536]{1,0:T(8,128)(2,1)}, bf16[72,1536]{1,0:T(8,128)(2,1)}, u32[]{:S(2)}, u32[]{:S(2)}) collective-permute-start(bf16[72,1536]{1,0:T(8,128)(2,1)} %collective-permute-done.8), channel_id=1, source_target_pairs={{0,2},{2,4},{4,6},{6,8},{8,10},{10,12},{12,14},{14,16},{16,18},{18... | collective-permute-start | bytes 663560 | tf_op jit(solution)/shard_map/ppermute | solution.py:107
  273.6 266.9 %copy-start.1 = (f32[512,1152]{1,0:T(8,128)}, f32[512,1152]{1,0:T(8,128)S(1)}, u32[]{:S(2)}) copy-start(f32[512,1152]{1,0:T(8,128)S(1)} %get-tuple-element.306) | copy-start | bytes 7077892
  275.7 261.8 %reduce-scatter.22.cloned.1.call-start = ((), (), s32[]{:S(2)}) async-start(), calls=%async_computation.26 | async-start | bytes 7077888 | tf_op jit(solution)/shard_map/reduce_scatter | solution.py:57
  279.0 12.6 collective-permute-start.13
  282.7 8.3 collective-permute-start.12
  291.0 8.1 collective-permute-start.14
  444.1 9.7 copy-start.49
  444.1 9.7 copy-start.54
  453.8 11.2 copy-start.47
  477.4 63.8 %copy-start.9 = (bf16[512,1152]{1,0:T(8,128)(2,1)S(1)}, bf16[512,1152]{1,0:T(8,128)(2,1)}, u32[]{:S(2)}) copy-start(bf16[512,1152]{1,0:T(8,128)(2,1)} %param.29) | copy-start | bytes 3538948
  477.4 102.3 %all-gather.23.cloned.1.call-start = ((), (), s32[]{:S(2)}) async-start(), calls=%async_computation.27 | async-start | bytes 3538944 | tf_op jit(solution)/shard_map/all_gather | solution.py:61
  584.6 19.8 %all-to-all-start.2 = ((bf16[2,512,576]{1,2,0:T(8,128)(2,1)}), bf16[2,512,576]{1,2,0:T(8,128)(2,1)}, u32[]{:S(2)}, u32[]{:S(2)}) async-start(bf16[2,512,576]{1,2,0:T(8,128)(2,1)} %bitcast.162), calls=%async_computation.5 | async-start | bytes 2359296 | tf_op jit(solution)/shard_map/all_to_all | solution.py:49
  589.1 201.4 %reduce-scatter.24.cloned.1.call-start = ((), (), s32[]{:S(2)}) async-start(), calls=%async_computation.28 | async-start | bytes 2359296 | tf_op jit(solution)/shard_map/reduce_scatter | solution.py:314
  607.2 125.1 %copy-start.26 = (f32[1024]{0:T(1024)S(1)}, f32[1024]{0:T(1024)}, u32[]{:S(2)}) copy-start(f32[1024]{0:T(1024)} %copy-done.24) | copy-start | bytes 12292
  607.2 125.1 %copy-start.36 = (f32[384]{0:T(512)S(1)}, f32[384]{0:T(512)}, u32[]{:S(2)}) copy-start(f32[384]{0:T(512)} %fusion.100) | copy-start | bytes 4612
  632.5 5.5 copy-start
  695.1 5.4 copy-start
  740.2 7.1 copy-start.12
  747.1 55.7 %reduce-scatter.26.cloned.1.call-start = ((), (), s32[]{:S(2)}) async-start(), calls=%async_computation.29 | async-start | bytes 2359296 | tf_op jit(solution)/shard_map/reduce_scatter | solution.py:315
  748.0 8.0 copy-start.4
  756.1 112.6 %reduce-scatter.28.cloned.1.call-start = ((), (), s32[]{:S(2)}) async-start(), calls=%async_computation.30 | async-start | bytes 7077888 | tf_op jit(solution)/shard_map/reduce_scatter | solution.py:57
  767.1 18.9 %copy-start.51 = (bf16[1152,576]{1,0:T(8,128)(2,1)S(1)}, bf16[1152,576]{1,0:T(8,128)(2,1)}, u32[]{:S(2)}) copy-start(bf16[1152,576]{1,0:T(8,128)(2,1)} %all-gather.11.cloned.1.call-done) | copy-start | bytes 3981316
  790.5 12.2 copy-start.14
  808.5 123.7 %reduce-scatter.20.cloned.1.call-start = ((), (), s32[]{:S(2)}) async-start(), calls=%async_computation.24 | async-start | bytes 7077888 | tf_op jit(solution)/shard_map/reduce_scatter | solution.py:57
  818.0 208.5 %reduce-scatter.38.cloned.1.call-start = ((), (), s32[]{:S(2)}) async-start(), calls=%async_computation.35 | async-start | bytes 7520256 | tf_op jit(solution)/shard_map/reduce_scatter | solution.py:347
  827.3 293.7 %reduce-scatter.34.cloned.1.call-start = ((), (), s32[]{:S(2)}) async-start(), calls=%async_computation.33 | async-start | bytes 7520256 | tf_op jit(solution)/shard_map/reduce_scatter | solution.py:345
  836.5 378.6 %reduce-scatter.36.cloned.1.call-start = ((), (), s32[]{:S(2)}) async-start(), calls=%async_computation.34 | async-start | bytes 7520256 | tf_op jit(solution)/shard_map/reduce_scatter | solution.py:346
  844.5 440.3 %reduce-scatter.42.cloned.1.call-start = ((), (), s32[]{:S(2)}) async-start(), calls=%async_computation.37 | async-start | bytes 3133440
  851.1 495.5 %reduce-scatter.32.cloned.1.call-start = ((), (), s32[]{:S(2)}) async-start(), calls=%async_computation.32 | async-start | bytes 1253376 | tf_op jit(solution)/shard_map/reduce_scatter | solution.py:343
  855.9 552.3 %reduce-scatter.30.cloned.1.call-start = ((), (), s32[]{:S(2)}) async-start(), calls=%async_computation.31 | async-start | bytes 1253376 | tf_op jit(solution)/shard_map/reduce_scatter | solution.py:342
  859.2 618.2 %reduce-scatter.40.cloned.1.call-start = ((), (), s32[]{:S(2)}) async-start(), calls=%async_computation.36 | async-start | bytes 3133440
  863.3 68.9 %copy-start.2 = (f32[512,1152]{1,0:T(8,128)S(1)}, f32[512,1152]{1,0:T(8,128)}, u32[]{:S(2)}) copy-start(f32[512,1152]{1,0:T(8,128)} %copy-done.1) | copy-start | bytes 7077892
  863.3 68.9 %copy-start.23 = (f32[1152]{0:T(1024)S(1)}, f32[1152]{0:T(1024)}, u32[]{:S(2)}) copy-start(f32[1152]{0:T(1024)} %convert_element_type.142) | copy-start | bytes 13828
  (34 other events, 87.6 us)
Sparse Core Ops, SparseCore 0:
  9.6 38.7 all-gather.8
  50.6 39.3 all-gather.10
  92.1 38.1 all-gather.12
  212.9 57.8 reduce-scatter.17
  272.3 36.0 all-gather.20
  310.8 47.1 all-gather.18
  360.6 46.1 all-gather.16
  409.0 35.0 all-gather.14
  477.5 59.9 reduce-scatter.21
  543.6 36.0 all-gather.22
  747.2 26.4 reduce-scatter.23
  775.8 26.8 reduce-scatter.25
  808.6 59.9 reduce-scatter.27
  870.9 61.2 reduce-scatter.19
  936.6 89.8 reduce-scatter.37
  1031.5 89.4 reduce-scatter.33
  1125.5 89.6 reduce-scatter.35
  1220.0 64.7 reduce-scatter.41
  1289.4 57.1 reduce-scatter.31
  1351.0 57.0 reduce-scatter.29
  1413.2 64.2 reduce-scatter.39
